TPU v7x, 256 devices: a whole 4x4x8 slice. The times are simulated.
256 devices in a mesh: rows: 8 (over x, core), protos: 32 (over y, z).
Axes of the slice: x: 4, y: 4, z: 8, core: 2. Of those that a mesh axis runs over, the one named last changes fastest.
Arguments:
- teacher_features: bfloat16 [4096, 384], P(('rows', 'protos')), may hold values from -80 to 80, as said below
- student_features: bfloat16 [4096, 384], P(('rows', 'protos')), may hold values from -80 to 80, as said below
- prototypes: bfloat16 [131072, 384], P('protos'), may hold values from -80 to 80, as said below
Outputs:
- feature_grad: float32 [4096, 384], P(('rows', 'protos'))
- proto_grad: float32 [8, 16384, 384], P('rows', 'protos')
Inputs may be any that keep to these rules, and one draw needn't show every extreme that they name: `teacher_features`: every row has nonzero entries. `student_features`: every row has nonzero entries. `prototypes`: every row has nonzero entries.
All inputs are finite; a program needn't handle non-finite values.
Results may differ from a plain program's by a relative error of at most 0.012.
The roundings to bfloat16 on the way count: a program that leaves them out, or rounds other values in their place, can miss the bound.
Values may be sent and summed in bfloat16 or wider, within the bound.
A program may use at most 64 MiB of HBM per device.

v0:
```python
import math
import jax
import jax.numpy as jnp
from jax import lax
from jax.sharding import PartitionSpec as P

D = 384
K = 131072
PASSES = 3
eps = 1e-06


def unitize(values):
    values = values.astype(jnp.float32)
    return (values * lax.rsqrt(jnp.sum(values * values, axis=1, keepdims=True) + eps)).astype(
        jnp.bfloat16
    )


def against(left, right):
    return lax.dot_general(
        left, right, (((1,), (1,)), ((), ())), preferred_element_type=jnp.float32
    )


def on_device(teacher_features, student_features, prototypes):
    scale = 1.5 * math.sqrt(D)
    unit_w = unitize(prototypes)
    local_t = unitize(teacher_features)
    local_s = unitize(student_features)
    unit_t, unit_s = (
        lax.all_gather(local_t, "protos", axis=0, tiled=True),
        lax.all_gather(local_s, "protos", axis=0, tiled=True),
    )
    kernel = jnp.exp(scale * against(unit_t, unit_w))
    powers = jnp.exp(scale * against(unit_s, unit_w))
    student_part = jnp.sum(powers, axis=1)
    student_whole = lax.psum(student_part, "protos")
    row_scale = jnp.ones((kernel.shape[0],), jnp.float32)
    col_scale = jnp.ones((kernel.shape[1],), jnp.float32)
    for step in range(PASSES):
        col_part = jnp.dot(row_scale, kernel, precision=lax.Precision.HIGHEST)
        col_scale = 1.0 / lax.psum(col_part, "rows")
        row_part = jnp.dot(kernel, col_scale, precision=lax.Precision.HIGHEST)
        if step == 0:
            row_whole = lax.psum(row_part, "protos")
        else:
            row_whole = lax.psum(row_part, "protos")
        row_scale = 1.0 / row_whole
    target = kernel * row_scale[:, None] * col_scale[None, :]
    probs = powers / student_whole[:, None]
    delta = (probs - target).astype(jnp.bfloat16)
    feature_term = scale * jnp.dot(delta, unit_w, preferred_element_type=jnp.float32)
    feature_grad = lax.psum_scatter(feature_term, "protos", scatter_dimension=0, tiled=True)
    row_groups = lax.axis_size("rows")
    total_rows = delta.shape[0] * row_groups
    factor = scale * K / total_rows
    block = delta.shape[1] // row_groups
    term = factor * lax.dot_general(
        delta, unit_s, (((0,), (0,)), ((), ())), preferred_element_type=jnp.float32
    )
    proto_grad = lax.psum_scatter(
        term.reshape(row_groups, block, term.shape[1]), "rows", scatter_dimension=0, tiled=True
    )
    return (feature_grad, proto_grad)


def solution(mesh):
    return jax.shard_map(
        on_device,
        mesh=mesh,
        in_specs=(P(("rows", "protos"), None), P(("rows", "protos"), None), P("protos", None)),
        out_specs=(P(("rows", "protos"), None), P("rows", "protos", None)),
        check_vma=False,
    )
```

profile of v0, /device:TPU:1, one launch (start us, length us, event | category | flops | bytes accessed | tf_op | source)
XLA Modules:
  0.0 735.6 jit_solution(5828482277272511359)
XLA Ops:
  7.2 0.0 reduce-scatter.3.cloned.1.call-start
  7.2 0.8 fusion.5
  8.0 0.8 fusion.3
  8.9 0.8 fusion.4
  9.7 0.8 fusion.6
  10.4 2.6 fusion.1
  13.1 41.6 %all_gather.6 = bf16[512,384]{1,0:T(8,128)(2,1)S(1)} all-gather(bf16[16,384]{1,0:T(8,128)(2,1)S(1)} %fusion.4), channel_id=1, replica_groups=mesh['rows'=8,'protos'=32] {'protos'}, dimensions={0}, use_global_device_ids=true | all-gather | bytes 405504 | tf_op jit(solution)/shard_map/all_gather | solution.py:33
  54.6 36.7 %all_gather.7 = bf16[512,384]{1,0:T(8,128)(2,1)S(1)} all-gather(bf16[16,384]{1,0:T(8,128)(2,1)S(1)} %fusion.6), channel_id=1, replica_groups=mesh['rows'=8,'protos'=32] {'protos'}, dimensions={0}, use_global_device_ids=true | all-gather | bytes 405504 | tf_op jit(solution)/shard_map/all_gather | solution.py:32
  91.3 4.3 multiply_exponential_fusion
  95.7 3.2 copy-done
  98.9 4.0 fusion.7
  102.9 44.7 %psum.50 = f32[4096]{0:T(1024)S(1)} all-reduce(f32[4096]{0:T(1024)S(1)} %bitcast.34), channel_id=1, replica_groups=mesh['rows'=8,'protos'=32] {'rows'}, use_global_device_ids=true, to_apply=%region_5.0 | all-reduce | flops 4096 | bytes 32768 | tf_op jit(solution)/shard_map/psum | solution.py:43
  147.7 9.4 %fusion.14 = f32[1,512]{1,0:T(1,128)S(1)} fusion(f32[512,4096]{1,0:T(8,128)} %copy-done, f32[4096,1]{0,1:T(1,128)S(1)} %bitcast.30), kind=kOutput, calls=%fused_computation.31 | convolution fusion | flops 25165824 | bytes 8407040 | tf_op jit(solution)/shard_map/dot_general | solution.py:44
  157.1 58.6 %psum.51 = f32[512]{0:T(512)S(1)} all-reduce(f32[512]{0:T(512)S(1)} %bitcast.36), channel_id=1, replica_groups=mesh['rows'=8,'protos'=32] {'protos'}, use_global_device_ids=true, to_apply=%region_6.0 | all-reduce | flops 512 | bytes 4096 | tf_op jit(solution)/shard_map/psum | solution.py:46
  215.7 6.3 fusion.15
  222.1 37.4 %psum.52 = f32[4096]{0:T(1024)S(1)} all-reduce(f32[4096]{0:T(1024)S(1)} %bitcast.31), channel_id=1, replica_groups=mesh['rows'=8,'protos'=32] {'rows'}, use_global_device_ids=true, to_apply=%region_7.0 | all-reduce | flops 4096 | bytes 32768 | tf_op jit(solution)/shard_map/psum | solution.py:43
  259.5 9.4 %fusion.16 = f32[1,512]{1,0:T(1,128)S(1)} fusion(f32[512,4096]{1,0:T(8,128)} %copy-done, f32[4096,1]{0,1:T(1,128)S(1)} %bitcast.32), kind=kOutput, calls=%fused_computation.33 | convolution fusion | flops 25165824 | bytes 8407040 | tf_op jit(solution)/shard_map/dot_general | solution.py:44
  268.9 55.8 %psum.53 = f32[512]{0:T(512)S(1)} all-reduce(f32[512]{0:T(512)S(1)} %bitcast.38), channel_id=1, replica_groups=mesh['rows'=8,'protos'=32] {'protos'}, use_global_device_ids=true, to_apply=%region_8.0 | all-reduce | flops 512 | bytes 4096 | tf_op jit(solution)/shard_map/psum | solution.py:48
  324.7 6.5 fusion.17
  331.2 37.6 %psum.54 = f32[4096]{0:T(1024)} all-reduce(f32[4096]{0:T(1024)S(1)} %bitcast.33), channel_id=1, replica_groups=mesh['rows'=8,'protos'=32] {'rows'}, use_global_device_ids=true, to_apply=%region_9.0 | all-reduce | flops 4096 | bytes 32768 | tf_op jit(solution)/shard_map/psum | solution.py:43
  368.8 0.7 broadcast_divide_fusion
  369.6 10.0 %fusion.18 = f32[1,512]{1,0:T(1,128)} fusion(f32[512,4096]{1,0:T(8,128)} %copy-done, f32[4096,1]{0,1:T(1,128)S(1)} %bitcast.29), kind=kOutput, calls=%fused_computation.35 | convolution fusion | flops 25165824 | bytes 8407040 | tf_op jit(solution)/shard_map/dot_general | solution.py:44
  379.6 6.2 fusion
  385.8 58.2 %all-reduce = (f32[512]{0:T(512)}, f32[512]{0:T(512)}) all-reduce(f32[512]{0:T(512)} %bitcast.35, f32[512]{0:T(512)} %get-tuple-element.4), channel_id=1, replica_groups=mesh['rows'=8,'protos'=32] {'protos'}, use_global_device_ids=true, to_apply=%region_10.0 | all-reduce | flops 1024 | bytes 8192 | tf_op jit(solution)/shard_map/psum | solution.py:48
  444.0 0.7 broadcast_divide_fusion.5
  444.6 7.3 subtract_convert_fusion
  452.0 2.0 copy-done.2
  454.0 3.3 convolution_multiply_fusion.1
  457.4 0.0 reduce-scatter.5.cloned.1.call-start
  457.4 7.2 convolution_multiply_fusion
  464.7 212.9 %reduce-scatter.3.cloned.1.call-done = f32[16,384]{1,0:T(8,128)} async-done(((f32[512,384]{1,0:T(8,128)}), f32[16,384]{1,0:T(8,128)}) %reduce-scatter.3.cloned.1.call-update) | async-done | bytes 24592 | tf_op jit(solution)/shard_map/reduce_scatter | solution.py:54
  677.6 51.2 %reduce-scatter.5.cloned.1.call-done = f32[1,512,384]{2,1,0:T(8,128)} async-done(((f32[8,512,384]{2,1,0:T(8,128)}), f32[1,512,384]{2,1,0:T(8,128)}) %reduce-scatter.5.cloned.1.call-update) | async-done | bytes 786448 | tf_op jit(solution)/shard_map/reduce_scatter | solution.py:62
  (17 shorter events, 0.1 us)
Async XLA Ops:
  7.2 670.4 %reduce-scatter.3.cloned.1.call-start = ((), (), s32[]{:S(2)}) async-start(), calls=%async_computation.2 | async-start | bytes 811008 | tf_op jit(solution)/shard_map/reduce_scatter | solution.py:54
  13.0 89.9 %copy-start.3 = (f32[4096]{0:T(1024)}, f32[4096]{0:T(1024)S(1)}, u32[]{:S(2)}) copy-start(f32[4096]{0:T(1024)S(1)} %add_rsqrt_fusion) | copy-start | bytes 49156
  95.7 3.2 copy-start
  324.7 54.9 %copy-start.1 = (bf16[4096,384]{1,0:T(8,128)(2,1)S(1)}, bf16[4096,384]{1,0:T(8,128)(2,1)}, u32[]{:S(2)}) copy-start(bf16[4096,384]{1,0:T(8,128)(2,1)} %param.5) | copy-start | bytes 9437188
  444.6 9.4 %copy-start.4 = (f32[4096]{0:T(1024)S(1)}, f32[4096]{0:T(1024)}, u32[]{:S(2)}) copy-start(f32[4096]{0:T(1024)} %copy-done.3) | copy-start | bytes 49156
  452.0 2.0 copy-start.2
  457.4 271.4 %reduce-scatter.5.cloned.1.call-start = ((), (), s32[]{:S(2)}) async-start(), calls=%async_computation.3 | async-start | bytes 7077888 | tf_op jit(solution)/shard_map/reduce_scatter | solution.py:62
Sparse Core Ops, SparseCore 0:
  457.5 220.0 reduce-scatter.2
  680.7 48.0 reduce-scatter.4
where the time goes:
time: 736 us
  blocking collectives  371 us (50%)
  waiting for transfers between devices  264 us (36%)
  matrix products  66.9 us (9%)
  other arithmetic  14.6 us (2%)
  between operations  14.1 us (2%)
    reduce_scatter x1, waiting for transfers between devices, on_device(): lax.psum_scatter(feature_term, 'protos', scatter_dimension=0, tiled=True)  213 us
    psum x3, blocking collectives, on_device(): row_whole = lax.psum(row_part, 'protos')  173 us
    psum x3, blocking collectives, on_device(): col_scale = 1.0 / lax.psum(col_part, 'rows')  120 us
    reduce_scatter x1, waiting for transfers between devices, on_device(): lax.psum_scatter(term.reshape(row_groups, block, term.shape[1]), 'rows',...  51.2 us
    all_gather x1, blocking collectives, on_device(): lax.all_gather(local_s, 'protos', axis=0, tiled=True)  41.6 us
    all_gather x1, blocking collectives, on_device(): lax.all_gather(local_t, 'protos', axis=0, tiled=True)  36.7 us
    dot_general x3, matrix products, on_device(): row_part = jnp.dot(kernel, col_scale, precision=lax.Precision.HIGHEST)  28.9 us
    dot_general x3, matrix products, on_device(): col_part = jnp.dot(row_scale, kernel, precision=lax.Precision.HIGHEST)  16.9 us
  transfers between devices with their start and end apart: 2, of which 2 were waited for; matrix products, arithmetic and copies ran while one was open for 1% of the time, Pallas kernels for 0%

commit v1 on v0

--- a/solution.py
+++ b/solution.py
@@ -45,7 +45,8 @@
         if step == 0:
             row_whole = lax.psum(row_part, "protos")
         else:
-            row_whole = lax.psum(row_part, "protos")
+            parts = lax.all_gather(row_part, "protos")
+            row_whole = jnp.sum(parts, axis=0)
         row_scale = 1.0 / row_whole
     target = kernel * row_scale[:, None] * col_scale[None, :]
     probs = powers / student_whole[:, None]

time: 736 us -> 705 us (0.958)
  blocking collectives: 371 us -> 335 us
    psum x3 -> x1, blocking collectives: 173 us -> 58.8 us  [on_device(): row_whole = lax.psum(row_part, 'protos')]
    all_gather x0 -> x2, blocking collectives: none -> 77.2 us  [on_device(): parts = lax.all_gather(row_part, 'protos')]
where the time goes in v1:
time: 705 us; the launch traced here: 704 us
  blocking collectives  335 us (48%)
  waiting for transfers between devices  265 us (38%)
  matrix products  66.6 us (9%)
  other arithmetic  18.4 us (3%)
  between operations  14.1 us (2%)
    reduce_scatter x1, waiting for transfers between devices, on_device(): lax.psum_scatter(feature_term, 'protos', scatter_dimension=0, tiled=True)  214 us
    psum x3, blocking collectives, on_device(): col_scale = 1.0 / lax.psum(col_part, 'rows')  120 us
    all_gather x2, blocking collectives, on_device(): parts = lax.all_gather(row_part, 'protos')  77.2 us
    psum x1, blocking collectives, on_device(): row_whole = lax.psum(row_part, 'protos')  58.8 us
    reduce_scatter x1, waiting for transfers between devices, on_device(): lax.psum_scatter(term.reshape(row_groups, block, term.shape[1]), 'rows',...  51.2 us
    all_gather x1, blocking collectives, on_device(): lax.all_gather(local_s, 'protos', axis=0, tiled=True)  41.6 us
    all_gather x1, blocking collectives, on_device(): lax.all_gather(local_t, 'protos', axis=0, tiled=True)  36.7 us
    dot_general x3, matrix products, on_device(): row_part = jnp.dot(kernel, col_scale, precision=lax.Precision.HIGHEST)  28.9 us
  transfers between devices with their start and end apart: 2, of which 2 were waited for; matrix products, arithmetic and copies ran while one was open for 1% of the time, Pallas kernels for 0%

profile of v1, /device:TPU:1, one launch (start us, length us, event | category | flops | bytes accessed | tf_op | source)
XLA Modules:
  0.0 704.2 jit_solution(11898373398884908829)
XLA Ops:
  7.2 0.8 fusion.5
  8.0 0.8 fusion.3
  8.9 0.8 fusion.4
  9.7 0.8 fusion.6
  10.4 2.6 fusion.1
  13.1 41.6 %all_gather.18 = bf16[512,384]{1,0:T(8,128)(2,1)S(1)} all-gather(bf16[16,384]{1,0:T(8,128)(2,1)S(1)} %fusion.4), channel_id=1, replica_groups=mesh['rows'=8,'protos'=32] {'protos'}, dimensions={0}, use_global_device_ids=true | all-gather | bytes 405504 | tf_op jit(solution)/shard_map/all_gather | solution.py:33
  54.6 36.7 %all_gather.19 = bf16[512,384]{1,0:T(8,128)(2,1)S(1)} all-gather(bf16[16,384]{1,0:T(8,128)(2,1)S(1)} %fusion.6), channel_id=1, replica_groups=mesh['rows'=8,'protos'=32] {'protos'}, dimensions={0}, use_global_device_ids=true | all-gather | bytes 405504 | tf_op jit(solution)/shard_map/all_gather | solution.py:32
  91.3 4.3 multiply_exponential_fusion
  95.7 3.2 copy-done
  98.9 4.6 fusion.7
  103.5 45.3 %psum.36 = f32[4096]{0:T(1024)} all-reduce(f32[4096]{0:T(1024)} %bitcast.40), channel_id=1, replica_groups=mesh['rows'=8,'protos'=32] {'rows'}, use_global_device_ids=true, to_apply=%region_5.0 | all-reduce | flops 4096 | bytes 32768 | tf_op jit(solution)/shard_map/psum | solution.py:43
  148.9 0.7 broadcast_divide_fusion.2
  149.6 10.0 %fusion.14 = f32[1,512]{1,0:T(1,128)} fusion(f32[512,4096]{1,0:T(8,128)} %copy-done, f32[4096,1]{0,1:T(1,128)S(1)} %bitcast.36), kind=kOutput, calls=%fused_computation.33 | convolution fusion | flops 25165824 | bytes 8407040 | tf_op jit(solution)/shard_map/dot_general | solution.py:44
  159.6 5.5 fusion
  165.1 58.8 %all-reduce = (f32[512]{0:T(512)S(1)}, f32[512]{0:T(512)}) all-reduce(f32[512]{0:T(512)} %bitcast.41, f32[512]{0:T(512)} %get-tuple-element.4), channel_id=1, replica_groups=mesh['rows'=8,'protos'=32] {'protos'}, use_global_device_ids=true, to_apply=%region_6.0 | all-reduce | flops 1024 | bytes 8192 | tf_op jit(solution)/shard_map/psum | solution.py:46
  223.9 6.3 fusion.15
  230.3 38.3 %psum.38 = f32[4096]{0:T(1024)} all-reduce(f32[4096]{0:T(1024)S(1)} %bitcast.37), channel_id=1, replica_groups=mesh['rows'=8,'protos'=32] {'rows'}, use_global_device_ids=true, to_apply=%region_7.0 | all-reduce | flops 4096 | bytes 32768 | tf_op jit(solution)/shard_map/psum | solution.py:43
  268.6 0.7 broadcast_divide_fusion.1
  269.3 9.4 %convolution_bitcast_fusion.1 = f32[1,1,512]{2,1,0:T(1,128)S(1)} fusion(f32[512,4096]{1,0:T(8,128)} %copy-done, f32[4096,1]{0,1:T(1,128)S(1)} %bitcast.38), kind=kOutput, calls=%fused_computation.11 | convolution fusion | flops 25165824 | bytes 8407040 | tf_op jit(solution)/shard_map/dot_general | solution.py:44
  278.7 37.8 %all-gather.2 = f32[32,1,512]{2,1,0:T(1,128)} all-gather(f32[1,1,512]{2,1,0:T(1,128)S(1)} %convolution_bitcast_fusion.1), channel_id=2, replica_groups=mesh['rows'=8,'protos'=32] {'protos'}, dimensions={0}, use_global_device_ids=true | all-gather | bytes 67584 | tf_op jit(solution)/shard_map/all_gather | solution.py:48
  316.6 0.9 reduce_sum.58
  317.5 6.3 fusion.16
  323.8 36.6 %psum.39 = f32[4096]{0:T(1024)} all-reduce(f32[4096]{0:T(1024)S(1)} %bitcast.39), channel_id=1, replica_groups=mesh['rows'=8,'protos'=32] {'rows'}, use_global_device_ids=true, to_apply=%region_9.0 | all-reduce | flops 4096 | bytes 32768 | tf_op jit(solution)/shard_map/psum | solution.py:43
  361.2 9.4 %convolution_bitcast_fusion = f32[1,1,512]{2,1,0:T(1,128)S(1)} fusion(f32[512,4096]{1,0:T(8,128)} %copy-done, f32[4096,1]{0,1:T(1,128)S(1)} %bitcast.35), kind=kOutput, calls=%fused_computation.10 | convolution fusion | flops 25165824 | bytes 8407040 | tf_op jit(solution)/shard_map/dot_general | solution.py:44
  370.6 39.4 %all-gather.3 = f32[32,1,512]{2,1,0:T(1,128)} all-gather(f32[1,1,512]{2,1,0:T(1,128)S(1)} %convolution_bitcast_fusion), channel_id=3, replica_groups=mesh['rows'=8,'protos'=32] {'protos'}, dimensions={0}, use_global_device_ids=true | all-gather | bytes 67584 | tf_op jit(solution)/shard_map/all_gather | solution.py:48
  410.0 1.5 reduce_sum.59
  412.1 7.3 %subtract_convert_fusion = bf16[512,4096]{1,0:T(8,128)(2,1)S(1)} fusion(f32[512,4096]{1,0:T(8,128)} %copy-done, f32[512,4096]{1,0:T(8,128)} %get-tuple-element.5, f32[4096]{0:T(1024)S(1)} %broadcast_divide_fusion, f32[512]{0:T(512)S(1)} %broadcast_divide_fusion.5, f32[512]{0:T(512)} %get-tuple-element.3), kind=kLoop, calls=%fused_computation | loop fusion | flops 12582912 | bytes 20992000 | tf_op jit(solution)/shard_map/convert_element_type | solution.py:53
  419.5 2.0 copy-done.2
  421.5 3.3 convolution_multiply_fusion.1
  424.9 7.2 %convolution_multiply_fusion = f32[4096,384]{1,0:T(8,128)} fusion(bf16[512,4096]{1,0:T(8,128)(2,1)} %copy-done.2, bf16[512,384]{1,0:T(8,128)(2,1)S(1)} %all_gather.18), kind=kOutput, calls=%fused_computation.8 | convolution fusion | flops 1612185600 | bytes 10878976 | tf_op jit(solution)/shard_map/dot_general | solution.py:60
  432.2 214.1 %reduce-scatter.3.cloned.1.call-done = f32[16,384]{1,0:T(8,128)} async-done(((f32[512,384]{1,0:T(8,128)}), f32[16,384]{1,0:T(8,128)}) %reduce-scatter.3.cloned.1.call-update) | async-done | bytes 24592 | tf_op jit(solution)/shard_map/reduce_scatter | solution.py:55
  646.2 51.2 %reduce-scatter.5.cloned.1.call-done = f32[1,512,384]{2,1,0:T(8,128)} async-done(((f32[8,512,384]{2,1,0:T(8,128)}), f32[1,512,384]{2,1,0:T(8,128)}) %reduce-scatter.5.cloned.1.call-update) | async-done | bytes 786448 | tf_op jit(solution)/shard_map/reduce_scatter | solution.py:63
  (19 shorter events, 1.6 us)
Async XLA Ops:
  7.2 639.0 %reduce-scatter.3.cloned.1.call-start = ((), (), s32[]{:S(2)}) async-start(), calls=%async_computation.2 | async-start | bytes 811008 | tf_op jit(solution)/shard_map/reduce_scatter | solution.py:55
  13.0 146.6 %copy-start.3 = (f32[4096]{0:T(1024)}, f32[4096]{0:T(1024)S(1)}, u32[]{:S(2)}) copy-start(f32[4096]{0:T(1024)S(1)} %add_rsqrt_fusion) | copy-start | bytes 49156
  95.7 3.2 copy-start
  98.9 60.7 %copy-start.1 = (bf16[4096,384]{1,0:T(8,128)(2,1)S(1)}, bf16[4096,384]{1,0:T(8,128)(2,1)}, u32[]{:S(2)}) copy-start(bf16[4096,384]{1,0:T(8,128)(2,1)} %param.5) | copy-start | bytes 9437188
  412.1 9.4 %copy-start.4 = (f32[4096]{0:T(1024)S(1)}, f32[4096]{0:T(1024)}, u32[]{:S(2)}) copy-start(f32[4096]{0:T(1024)} %copy-done.3) | copy-start | bytes 49156
  419.5 2.0 copy-start.2
  424.9 272.5 %reduce-scatter.5.cloned.1.call-start = ((), (), s32[]{:S(2)}) async-start(), calls=%async_computation.3 | async-start | bytes 7077888 | tf_op jit(solution)/shard_map/reduce_scatter | solution.py:63
Sparse Core Ops, SparseCore 0:
  425.0 221.1 reduce-scatter.2
  649.3 48.0 reduce-scatter.4
